TPU v7x, 256 devices: a whole 4x4x8 slice. The times are simulated.
256 devices in a mesh: wide: 64 (over z, x, core), slab: 4 (over y).
Axes of the slice: x: 4, y: 4, z: 8, core: 2. Of those that a mesh axis runs over, the one named last changes fastest.
Arguments:
- fields: float32 [4, 512, 512, 512], P(None, 'slab', 'wide'), may hold values from -60 to 60
- start_basis: float32 [512, 128], replicated, may hold values from -6 to 6
Outputs:
- core_tensor: float32 [4, 512, 512, 128], P(None, None, ('wide', 'slab'))
All inputs are finite; a program needn't handle non-finite values.
Results may differ from a plain program's by a relative error of at most 0.0003.
Values sent between devices are 32-bit elements; how exact they have to be, the bound alone decides.
A program may use at most 64 MiB of HBM per device.

v0:
```python
import functools

import jax
import jax.numpy as jnp
from jax import lax
from jax.experimental import pallas as pl
from jax.experimental.pallas import tpu as pltpu
from jax.sharding import PartitionSpec as P

SWEEPS = 4
MESH = pl.DeviceIdType.MESH
CORES, XS, ZS, YS = 2, 4, 8, 4
PLANE = XS * YS
N1 = 512
TILE = 128
PAIRS = [(i, j) for i in range(N1 // TILE) for j in range(i, N1 // TILE)]
HALF = len(PAIRS) // CORES
SHARE = HALF * TILE // PLANE
CHUNK = 512
SUB = 8
RANK = 128
HIGHEST = lax.Precision.HIGHEST
NT = (((1,), (1,)), ((), ()))
TN = (((0,), (0,)), ((), ()))
NN = (((1,), (0,)), ((), ()))


def inverse_factor(square, n):
    blocks = n // SUB
    lane = lax.broadcasted_iota(jnp.int32, (SUB, n), 1)
    sub = lax.broadcasted_iota(jnp.int32, (SUB, n), 0)
    a = [square[SUB * i:SUB * (i + 1), :] for i in range(blocks)]
    j = [(lane == sub + SUB * i).astype(jnp.float32) for i in range(blocks)]
    rows = []

    def along_lanes(v, c):
        return jnp.broadcast_to(v[:, c:c + 1], (SUB, n))

    def along_sublanes(v, p):
        return jnp.broadcast_to(v[p:p + 1, :], (SUB, n))

    for k in range(blocks):
        cols = [along_lanes(a[k], SUB * k + p) for p in range(SUB)]
        e = {(i, p): along_sublanes(cols[p], i) for p in range(SUB) for i in range(p, SUB)}
        r, l = [], {}
        for p in range(SUB):
            r.append(lax.rsqrt(e[p, p]))
            for i in range(p + 1, SUB):
                l[i, p] = e[i, p] * r[p]
            for q in range(p + 1, SUB):
                for i in range(q, SUB):
                    e[i, q] = e[i, q] - l[i, p] * l[q, p]

        def forward(values):
            out = []
            for p in range(SUB):
                v = values[p]
                for q in range(p):
                    v = v - l[p, q] * out[q]
                out.append(v * r[p])
            return out

        upper = forward([along_sublanes(a[k], p) for p in range(SUB)])
        inverse = forward([along_sublanes(j[k], p) for p in range(SUB)])
        rows.extend(v[:1] for v in inverse)
        for i in range(k + 1, blocks):
            lower = forward([along_lanes(a[i], SUB * k + p) for p in range(SUB)])
            for p in range(SUB):
                a[i] = a[i] - lower[p] * upper[p]
                j[i] = j[i] - lower[p] * inverse[p]
    return rows


def tucker_kernel(nv, x_hbm, start_ref, out_ref, xbuf, high_ref, low_ref, g_ref, basis_ref, product_ref, outbox, s_ref, mine, theirs, inbox, total, parts, zparts, load_sem, core_sem, rs_send, rs_recv, z_send, z_recv,
                ag_send, ag_recv, out_send, out_recv):
    wide = lax.axis_index("wide")
    y = lax.axis_index("slab")
    core = wide % CORES
    x = (wide // CORES) % XS
    z = wide // (CORES * XS)
    me = x * YS + y
    sibling = (wide + 1 - 2 * core, y)

    def plane_device(p):
        return ((z * XS + p // YS) * CORES + core, p % YS)

    def z_device(q):
        return ((q * XS + x) * CORES + core, y)

    barrier = pltpu.get_barrier_semaphore()
    pl.semaphore_signal(barrier, inc=1, device_id=sibling, device_id_type=MESH)
    for d in range(1, PLANE):
        pl.semaphore_signal(barrier, inc=1, device_id=plane_device((me + d) % PLANE), device_id_type=MESH)
    for d in range(1, ZS):
        pl.semaphore_signal(barrier, inc=1, device_id=z_device((z + d) % ZS), device_id_type=MESH)

    rows = x_hbm.shape[0]
    steps = rows // CHUNK

    def load(c):
        return pltpu.make_async_copy(x_hbm.at[pl.ds(c * CHUNK, CHUNK)], xbuf.at[pl.ds(c * CHUNK, CHUNK)], load_sem.at[c])

    for c in range(steps):
        load(c).start()
    s_ref[...] = jnp.zeros_like(s_ref)

    @pl.loop(0, steps)
    def _(c):
        load(c).wait()
        rows_ = pl.ds(pl.multiple_of(c * CHUNK, CHUNK), CHUNK)
        value = xbuf[rows_, :]
        high = value.astype(jnp.bfloat16)
        low = (value - high.astype(jnp.float32)).astype(jnp.bfloat16)
        high_ref[rows_, :] = high
        low_ref[rows_, :] = low
        s_ref[...] += 0.5 * lax.dot_general(high, high, TN, preferred_element_type=jnp.float32) + lax.dot_general(
            high, low, TN, preferred_element_type=jnp.float32)

    basis_ref[...] = start_ref[...].T
    scale = 1.0 / (rows * PLANE * ZS * CORES)
    pl.semaphore_wait(barrier, PLANE + ZS - 1)

    def block(n):
        i, j = PAIRS[n]
        a = s_ref[i * TILE:(i + 1) * TILE, j * TILE:(j + 1) * TILE]
        b = s_ref[j * TILE:(j + 1) * TILE, i * TILE:(i + 1) * TILE]
        return (a + b.T) * scale

    for c in range(CORES):
        @pl.when(core == c)
        def _():
            for n in range(HALF):
                theirs[n * TILE:(n + 1) * TILE, :] = block((1 - c) * HALF + n)
                mine[n * TILE:(n + 1) * TILE, :] = block(c * HALF + n)

    swap = pltpu.make_async_remote_copy(theirs, inbox, core_sem.at[0], core_sem.at[1], device_id=sibling, device_id_type=MESH)
    swap.start()
    swap.wait()
    mine[...] += inbox[...]

    def scatter(p, source):
        return pltpu.make_async_remote_copy(
            mine.at[pl.ds(p * SHARE, SHARE)], parts.at[source], rs_send.at[p], rs_recv.at[source],
            device_id=plane_device(p), device_id_type=MESH)

    @pl.loop(1, PLANE)
    def _(d):
        scatter((me + d) % PLANE, me).start()

    own = zparts.at[z]
    own[...] = mine[pl.ds(pl.multiple_of(me * SHARE, 8), SHARE), :]

    @pl.loop(1, PLANE)
    def _(d):
        source = (me + PLANE - d) % PLANE
        scatter((me + d) % PLANE, source).wait_recv()
        own[...] += parts[source]

    def along_z(q, source):
        return pltpu.make_async_remote_copy(
            zparts.at[z], zparts.at[source], z_send.at[q], z_recv.at[source], device_id=z_device(q), device_id_type=MESH)

    for d in range(1, ZS):
        pltpu.make_async_remote_copy(
            zparts.at[z], zparts.at[z], z_send.at[(z + d) % ZS], z_recv.at[z], device_id=z_device((z + d) % ZS),
            device_id_type=MESH).start()
    for d in range(1, ZS):
        q = (z + d) % ZS
        pltpu.make_async_remote_copy(
            zparts.at[q], zparts.at[q], z_send.at[q], z_recv.at[q], device_id=z_device(q), device_id_type=MESH).wait_recv()
    value = zparts[0]
    for q in range(1, ZS):
        value = value + zparts[q]
    done = total.at[core]
    done[pl.ds(pl.multiple_of(me * SHARE, 8), SHARE), :] = value

    def gather(p, source):
        rows_ = pl.ds(source * SHARE, SHARE)
        return pltpu.make_async_remote_copy(
            done.at[rows_], done.at[rows_], ag_send.at[p], ag_recv.at[source], device_id=plane_device(p), device_id_type=MESH)

    @pl.loop(1, PLANE)
    def _(d):
        gather((me + d) % PLANE, me).start()

    @pl.loop(1, PLANE)
    def _(d):
        source = (me + PLANE - d) % PLANE
        gather((me + d) % PLANE, source).wait_recv()

    back = pltpu.make_async_remote_copy(done, done, core_sem.at[2], core_sem.at[3], device_id=sibling, device_id_type=MESH)
    back.start()
    back.wait()

    for n, (i, j) in enumerate(PAIRS):
        m = n % HALF
        value = total[n // HALF, m * TILE:(m + 1) * TILE, :]
        g_ref[i * TILE:(i + 1) * TILE, j * TILE:(j + 1) * TILE] = value
        if i != j:
            g_ref[j * TILE:(j + 1) * TILE, i * TILE:(i + 1) * TILE] = value.T

    @pl.loop(0, SWEEPS)
    def _(sweep):
        block = lax.dot_general(basis_ref[...], g_ref[...], NN, precision=HIGHEST, preferred_element_type=jnp.float32)
        square = lax.dot_general(block, block, NT, precision=HIGHEST, preferred_element_type=jnp.float32)
        for n, row in enumerate(inverse_factor(square, RANK)):
            s_ref[n:n + 1, :RANK] = row
        basis_ref[...] = lax.dot_general(s_ref[:RANK, :RANK], block, NN, precision=HIGHEST, preferred_element_type=jnp.float32)

    basis = basis_ref[...]
    basis_high = basis.astype(jnp.bfloat16)
    basis_low = (basis - basis_high.astype(jnp.float32)).astype(jnp.bfloat16)
    both = jnp.concatenate([basis_high, basis_low], axis=0)
    pairs = CHUNK // YS
    halves = steps // nv

    def send(c, p, source):
        return pltpu.make_async_remote_copy(
            outbox.at[p, pl.ds(c * pairs, pairs)],
            out_ref.at[c // halves, pl.ds((source * halves + c % halves) * pairs, pairs)],
            out_send.at[c, p], out_recv.at[c, source], device_id=(wide, p), device_id_type=MESH)

    @pl.loop(0, steps)
    def _(c):
        rows_ = pl.ds(pl.multiple_of(c * CHUNK, CHUNK), CHUNK)
        wideproduct = lax.dot_general(high_ref[rows_, :], both, NT, preferred_element_type=jnp.float32)
        product_ref[...] = wideproduct[:, :RANK] + (wideproduct[:, RANK:] + lax.dot_general(
            low_ref[rows_, :], basis_high, NT, preferred_element_type=jnp.float32))
        width = 2 * YS
        count = CHUNK // width
        for p in range(YS):
            for i in range(2):
                outbox[p, pl.ds(c * pairs + i, count, stride=2), :] = product_ref[pl.ds(2 * p + i, count, stride=width), :]
        for d in (2, 1, 3):
            send(c, (y + d) % YS, y).start()
        out_ref[c // halves, pl.ds(pl.multiple_of((y * halves + c % halves) * pairs, pairs), pairs), :] = outbox[
            y, pl.ds(pl.multiple_of(c * pairs, pairs), pairs), :]

    @pl.loop(0, steps)
    def _(c):
        for d in (2, 1, 3):
            send(c, (y + d) % YS, (y + YS - d) % YS).wait_recv()

    @pl.loop(0, steps)
    def _(c):
        for d in (2, 1, 3):
            send(c, (y + d) % YS, y).wait_send()

    @pl.loop(1, PLANE)
    def _(d):
        p = (me + d) % PLANE
        scatter(p, me).wait_send()
        gather(p, me).wait_send()

    for d in range(1, ZS):
        q = (z + d) % ZS
        pltpu.make_async_remote_copy(
            zparts.at[z], zparts.at[z], z_send.at[q], z_recv.at[z], device_id=z_device(q), device_id_type=MESH).wait_send()


def per_device(fields, start_basis):
    nv, n2, n3, n1 = fields.shape
    unfolded = fields.reshape(-1, n1)
    rows = unfolded.shape[0]
    steps = rows // CHUNK
    out = pl.pallas_call(
        functools.partial(tucker_kernel, nv),
        out_shape=jax.ShapeDtypeStruct((nv, rows // nv, RANK), jnp.float32),
        in_specs=[pl.BlockSpec(memory_space=pl.ANY), pl.BlockSpec(memory_space=pltpu.VMEM)],
        out_specs=pl.BlockSpec(memory_space=pltpu.VMEM),
        scratch_shapes=[
            pltpu.VMEM((rows, n1), jnp.float32),
            pltpu.VMEM((rows, n1), jnp.bfloat16),
            pltpu.VMEM((rows, n1), jnp.bfloat16),
            pltpu.VMEM((n1, n1), jnp.float32),
            pltpu.VMEM((RANK, n1), jnp.float32),
            pltpu.VMEM((CHUNK, RANK), jnp.float32),
            pltpu.VMEM((YS, rows // YS, RANK), jnp.float32),
            pltpu.VMEM((n1, n1), jnp.float32),
            pltpu.VMEM((HALF * TILE, TILE), jnp.float32),
            pltpu.VMEM((HALF * TILE, TILE), jnp.float32),
            pltpu.VMEM((HALF * TILE, TILE), jnp.float32),
            pltpu.VMEM((CORES, HALF * TILE, TILE), jnp.float32),
            pltpu.VMEM((PLANE, SHARE, TILE), jnp.float32),
            pltpu.VMEM((ZS, SHARE, TILE), jnp.float32),
            pltpu.SemaphoreType.DMA((steps,)),
            pltpu.SemaphoreType.DMA((4,)),
            pltpu.SemaphoreType.DMA((PLANE,)),
            pltpu.SemaphoreType.DMA((PLANE,)),
            pltpu.SemaphoreType.DMA((ZS,)),
            pltpu.SemaphoreType.DMA((ZS,)),
            pltpu.SemaphoreType.DMA((PLANE,)),
            pltpu.SemaphoreType.DMA((PLANE,)),
            pltpu.SemaphoreType.DMA((steps, YS)),
            pltpu.SemaphoreType.DMA((steps, YS)),
        ],
        compiler_params=pltpu.CompilerParams(collective_id=0, has_side_effects=True, vmem_limit_bytes=56 << 20),
    )(unfolded, start_basis)
    return out.reshape(nv, n2 * YS, n3 // YS, RANK)


def solution(mesh):
    in_specs = (P(None, "slab", "wide", None), P())
    out_specs = P(None, None, ("wide", "slab"), None)
    return jax.shard_map(
        per_device, mesh=mesh, in_specs=in_specs, out_specs=out_specs, check_vma=False
    )
```

profile of v0, /device:TPU:1, one launch (start us, length us, event | category | flops | bytes accessed | tf_op | source)
XLA Modules:
  0.0 96.8 jit_solution(9423299057691323695)
XLA Ops:
  0.0 93.8 %shard_map.28 = f32[4,1024,128]{2,1,0:T(8,128)} custom-call(f32[4096,512]{1,0:T(8,128)} %bitcast.2, f32[512,128]{1,0:T(8,128)} %start_ref.1), custom_call_target="tpu_custom_call" | custom-call | tf_op jit(solution)/shard_map/pallas_call | solution.py:266
  93.8 3.0 %copy.4 = f32[4,512,2,128]{3,2,1,0:T(2,128)} copy(f32[4,512,2,128]{3,2,1,0:T(2,128)} %bitcast.3) | data formatting | bytes 4194304
where the time goes:
time: 97 us; the launch traced here: 96.8 us
  Pallas kernels  93.8 us (97%)
  local copies, waits for them, and re-layouts  3.05 us (3%)
    pallas_call x1, Pallas kernels, per_device(): pl.pallas_call(functools.partial(tucker_kernel, nv), out_shape=jax.ShapeD...  93.8 us
    unnamed x1, local copies, waits for them, and re-layouts  3.05 us

commit v1 on v0

v1 whole, which is shorter than its diff:
```python
import functools

import jax
import jax.numpy as jnp
from jax import lax
from jax.experimental import pallas as pl
from jax.experimental.pallas import tpu as pltpu
from jax.sharding import PartitionSpec as P

SWEEPS = 4
MESH = pl.DeviceIdType.MESH
CORES, XS, ZS, YS = 2, 4, 8, 4
PLANE = XS * YS
N1 = 512
TILE = 128
PAIRS = [(i, j) for i in range(N1 // TILE) for j in range(i, N1 // TILE)]
HALF = len(PAIRS) // CORES
OWN = TILE // PLANE
GROUPS = ((0, 3), (3, HALF))
CHUNK = 512
SUB = 8
RANK = 128
HIGHEST = lax.Precision.HIGHEST
NT = (((1,), (1,)), ((), ()))
TN = (((0,), (0,)), ((), ()))
NN = (((1,), (0,)), ((), ()))


def inverse_factor(square, n):
    blocks = n // SUB
    lane = lax.broadcasted_iota(jnp.int32, (SUB, n), 1)
    sub = lax.broadcasted_iota(jnp.int32, (SUB, n), 0)
    a = [square[SUB * i:SUB * (i + 1), :] for i in range(blocks)]
    j = [(lane == sub + SUB * i).astype(jnp.float32) for i in range(blocks)]
    rows = []

    def along_lanes(v, c):
        return jnp.broadcast_to(v[:, c:c + 1], (SUB, n))

    def along_sublanes(v, p):
        return jnp.broadcast_to(v[p:p + 1, :], (SUB, n))

    for k in range(blocks):
        cols = [along_lanes(a[k], SUB * k + p) for p in range(SUB)]
        e = {(i, p): along_sublanes(cols[p], i) for p in range(SUB) for i in range(p, SUB)}
        r, l = [], {}
        for p in range(SUB):
            r.append(lax.rsqrt(e[p, p]))
            for i in range(p + 1, SUB):
                l[i, p] = e[i, p] * r[p]
            for q in range(p + 1, SUB):
                for i in range(q, SUB):
                    e[i, q] = e[i, q] - l[i, p] * l[q, p]

        def forward(values):
            out = []
            for p in range(SUB):
                v = values[p]
                for q in range(p):
                    v = v - l[p, q] * out[q]
                out.append(v * r[p])
            return out

        upper = forward([along_sublanes(a[k], p) for p in range(SUB)])
        inverse = forward([along_sublanes(j[k], p) for p in range(SUB)])
        rows.extend(v[:1] for v in inverse)
        for i in range(k + 1, blocks):
            lower = forward([along_lanes(a[i], SUB * k + p) for p in range(SUB)])
            for p in range(SUB):
                a[i] = a[i] - lower[p] * upper[p]
                j[i] = j[i] - lower[p] * inverse[p]
    return rows


def tucker_kernel(nv, x_hbm, start_ref, y_ref, factor_ref, xbuf, g_ref, basis_ref, block_ref, last_ref, product_ref, outbox, s_ref, mine,
                  theirs, inbox, total, parts, zparts, load_sem, swap_sem, rs_send, rs_recv, z_send, z_recv, ag_send, ag_recv,
                  back_sem, out_send, out_recv, keep_sem):
    wide = lax.axis_index("wide")
    y = lax.axis_index("slab")
    core = wide % CORES
    x = (wide // CORES) % XS
    z = wide // (CORES * XS)
    me = x * YS + y
    sibling = (wide + 1 - 2 * core, y)
    groups = range(len(GROUPS))

    def plane_device(p):
        return ((z * XS + p // YS) * CORES + core, p % YS)

    def z_device(q):
        return ((q * XS + x) * CORES + core, y)

    barrier = pltpu.get_barrier_semaphore()
    pl.semaphore_signal(barrier, inc=1, device_id=sibling, device_id_type=MESH)

    @pl.loop(1, PLANE)
    def _(d):
        pl.semaphore_signal(barrier, inc=1, device_id=plane_device((me + d) % PLANE), device_id_type=MESH)

    @pl.loop(1, ZS)
    def _(d):
        pl.semaphore_signal(barrier, inc=1, device_id=z_device((z + d) % ZS), device_id_type=MESH)

    rows = x_hbm.shape[0]
    steps = rows // CHUNK

    def load(c):
        return pltpu.make_async_copy(x_hbm.at[pl.ds(c * CHUNK, CHUNK)], xbuf.at[pl.ds(c * CHUNK, CHUNK)], load_sem.at[c])

    for c in range(steps):
        load(c).start()
    s_ref[...] = jnp.zeros_like(s_ref)
    basis_ref[...] = start_ref[...].T

    @pl.loop(0, steps)
    def _(c):
        load(c).wait()
        value = xbuf[pl.ds(pl.multiple_of(c * CHUNK, CHUNK), CHUNK), :]
        high = value.astype(jnp.bfloat16)
        low = (value - high.astype(jnp.float32)).astype(jnp.bfloat16)
        s_ref[...] += 0.5 * lax.dot_general(high, high, TN, preferred_element_type=jnp.float32) + lax.dot_general(
            high, low, TN, preferred_element_type=jnp.float32)

    scale = 1.0 / (rows * PLANE * ZS * CORES)
    pl.semaphore_wait(barrier, PLANE + ZS - 1)

    def block(n):
        i, j = PAIRS[n]
        a = s_ref[i * TILE:(i + 1) * TILE, j * TILE:(j + 1) * TILE]
        b = s_ref[j * TILE:(j + 1) * TILE, i * TILE:(i + 1) * TILE]
        return (a + b.T) * scale

    def span(g):
        first, last = GROUPS[g]
        return pl.ds(first * TILE, (last - first) * TILE)

    def share(g):
        first, last = GROUPS[g]
        return pl.ds(first * OWN, (last - first) * OWN)

    def owned(g, p):
        first, last = GROUPS[g]
        return pl.ds(pl.multiple_of(first * TILE + p * ((last - first) * OWN), SUB), (last - first) * OWN)

    def swap(g):
        return pltpu.make_async_remote_copy(
            theirs.at[span(g)], inbox.at[span(g)], swap_sem.at[0, g], swap_sem.at[1, g], device_id=sibling, device_id_type=MESH)

    for g in groups:
        for c in range(CORES):
            @pl.when(core == c)
            def _():
                for n in range(*GROUPS[g]):
                    theirs[n * TILE:(n + 1) * TILE, :] = block((1 - c) * HALF + n)
        swap(g).start()
    for c in range(CORES):
        @pl.when(core == c)
        def _():
            for n in range(HALF):
                mine[n * TILE:(n + 1) * TILE, :] = block(c * HALF + n)

    def scatter(g, p, source):
        return pltpu.make_async_remote_copy(
            mine.at[owned(g, p)], parts.at[source, share(g)], rs_send.at[g, p], rs_recv.at[g, source],
            device_id=plane_device(p), device_id_type=MESH)

    def along_z(g, q, source):
        return pltpu.make_async_remote_copy(
            zparts.at[source, share(g)], zparts.at[source, share(g)], z_send.at[g, q], z_recv.at[g, source],
            device_id=z_device(q), device_id_type=MESH)

    done = total.at[core]

    def gather(g, p, source):
        return pltpu.make_async_remote_copy(
            done.at[owned(g, source)], done.at[owned(g, source)], ag_send.at[g, p], ag_recv.at[g, source],
            device_id=plane_device(p), device_id_type=MESH)

    def back(g, c):
        return pltpu.make_async_remote_copy(
            total.at[c, span(g)], total.at[c, span(g)], back_sem.at[0, g], back_sem.at[1, g], device_id=sibling, device_id_type=MESH)

    for g in groups:
        swap(g).wait_recv()
        mine[span(g), :] += inbox[span(g), :]

        @pl.loop(1, PLANE)
        def _(d):
            scatter(g, (me + d) % PLANE, me).start()

    for g in groups:
        zparts[z, share(g), :] = mine[owned(g, me), :]

        @pl.loop(1, PLANE)
        def _(d):
            source = (me + PLANE - d) % PLANE
            scatter(g, (me + d) % PLANE, source).wait_recv()
            zparts[z, share(g), :] += parts[source, share(g), :]

        @pl.loop(1, ZS)
        def _(d):
            along_z(g, (z + d) % ZS, z).start()

    for g in groups:
        @pl.loop(1, ZS)
        def _(d):
            along_z(g, (z + d) % ZS, (z + ZS - d) % ZS).wait_recv()

        value = zparts[0, share(g), :]
        for q in range(1, ZS):
            value = value + zparts[q, share(g), :]
        done[owned(g, me), :] = value

        @pl.loop(1, PLANE)
        def _(d):
            gather(g, (me + d) % PLANE, me).start()

    for g in groups:
        @pl.loop(1, PLANE)
        def _(d):
            gather(g, (me + d) % PLANE, (me + PLANE - d) % PLANE).wait_recv()

        back(g, core).start()

    for g in groups:
        back(g, 1 - core).wait_recv()
        for half in range(CORES):
            for m in range(*GROUPS[g]):
                i, j = PAIRS[half * HALF + m]
                value = total[half, m * TILE:(m + 1) * TILE, :]
                g_ref[i * TILE:(i + 1) * TILE, j * TILE:(j + 1) * TILE] = value
                if i != j:
                    g_ref[j * TILE:(j + 1) * TILE, i * TILE:(i + 1) * TILE] = value.T

    def times(a, b, dims):
        return lax.dot_general(a, b, dims, precision=HIGHEST, preferred_element_type=jnp.float32)

    def inverse_triangle(block_):
        for n, row in enumerate(inverse_factor(times(block_, block_, NT), RANK)):
            s_ref[n:n + 1, :RANK] = row
        return s_ref[:RANK, :RANK]

    @pl.loop(0, SWEEPS - 2)
    def _(sweep):
        block_ref[...] = times(basis_ref[...], g_ref[...], NN)
        basis_ref[...] = times(inverse_triangle(block_ref[...]), block_ref[...], NN)

    block_ref[...] = times(basis_ref[...], g_ref[...], NN)
    last_ref[...] = times(block_ref[...], g_ref[...], NN)
    pairs = CHUNK // YS
    halves = steps // nv

    def place(c, source):
        return y_ref.at[c // halves, pl.ds((source * halves + c % halves) * pairs, pairs)]

    def send(c, p, source):
        return pltpu.make_async_remote_copy(
            outbox.at[p, pl.ds(c * pairs, pairs)], place(c, source), out_send.at[c, p], out_recv.at[c, source],
            device_id=(wide, p), device_id_type=MESH)

    def keep(c):
        return pltpu.make_async_copy(outbox.at[y, pl.ds(c * pairs, pairs)], place(c, y), keep_sem.at[c])

    @pl.loop(0, steps)
    def _(c):
        product_ref[...] = times(xbuf[pl.ds(pl.multiple_of(c * CHUNK, CHUNK), CHUNK), :], last_ref[...], NT)
        width = 2 * YS
        count = CHUNK // width
        for p in range(YS):
            for i in range(2):
                outbox[p, pl.ds(c * pairs + i, count, stride=2), :] = product_ref[pl.ds(2 * p + i, count, stride=width), :]
        for d in (2, 1, 3):
            send(c, (y + d) % YS, y).start()
        keep(c).start()

    factor_ref[...] = jnp.zeros_like(factor_ref)

    @pl.loop(0, 2)
    def _(sweep):
        inverse = inverse_triangle(block_ref[...])

        @pl.when(sweep == 0)
        def _():
            factor_ref[...] = inverse
            block_ref[...] = times(inverse, last_ref[...], NN)

        @pl.when(sweep == 1)
        def _():
            factor_ref[...] = times(inverse, factor_ref[...], NN)

    for g in groups:
        swap(g).wait_send()
        back(g, core).wait_send()

        @pl.loop(1, PLANE)
        def _(d):
            p = (me + d) % PLANE
            scatter(g, p, me).wait_send()
            gather(g, p, me).wait_send()

        @pl.loop(1, ZS)
        def _(d):
            along_z(g, (z + d) % ZS, z).wait_send()

    @pl.loop(0, steps)
    def _(c):
        keep(c).wait()
        for d in (2, 1, 3):
            send(c, (y + d) % YS, y).wait_send()
            send(c, (y + d) % YS, (y + YS - d) % YS).wait_recv()


def finish_kernel(y_ref, factor_ref, out_hbm, out_ref, sem):
    nv = y_ref.shape[0]

    def store(v):
        return pltpu.make_async_copy(out_ref.at[v], out_hbm.at[v], sem.at[v])

    for v in range(nv):
        out_ref[v] = lax.dot_general(y_ref[v], factor_ref[...], NT, precision=HIGHEST, preferred_element_type=jnp.float32)
        store(v).start()
    for v in range(nv):
        store(v).wait()


def per_device(fields, start_basis):
    nv, n2, n3, n1 = fields.shape
    unfolded = fields.reshape(-1, n1)
    rows = unfolded.shape[0]
    steps = rows // CHUNK
    stages = len(GROUPS)
    y, factor = pl.pallas_call(
        functools.partial(tucker_kernel, nv),
        out_shape=[jax.ShapeDtypeStruct((nv, rows // nv, RANK), jnp.float32), jax.ShapeDtypeStruct((RANK, RANK), jnp.float32)],
        in_specs=[pl.BlockSpec(memory_space=pl.ANY), pl.BlockSpec(memory_space=pltpu.VMEM)],
        out_specs=[pl.BlockSpec(memory_space=pl.ANY), pl.BlockSpec(memory_space=pltpu.VMEM)],
        scratch_shapes=[
            pltpu.VMEM((rows, n1), jnp.float32),
            pltpu.VMEM((n1, n1), jnp.float32),
            pltpu.VMEM((RANK, n1), jnp.float32),
            pltpu.VMEM((RANK, n1), jnp.float32),
            pltpu.VMEM((RANK, n1), jnp.float32),
            pltpu.VMEM((CHUNK, RANK), jnp.float32),
            pltpu.VMEM((YS, rows // YS, RANK), jnp.float32),
            pltpu.VMEM((n1, n1), jnp.float32),
            pltpu.VMEM((HALF * TILE, TILE), jnp.float32),
            pltpu.VMEM((HALF * TILE, TILE), jnp.float32),
            pltpu.VMEM((HALF * TILE, TILE), jnp.float32),
            pltpu.VMEM((CORES, HALF * TILE, TILE), jnp.float32),
            pltpu.VMEM((PLANE, HALF * OWN, TILE), jnp.float32),
            pltpu.VMEM((ZS, HALF * OWN, TILE), jnp.float32),
            pltpu.SemaphoreType.DMA((steps,)),
            pltpu.SemaphoreType.DMA((2, stages)),
            pltpu.SemaphoreType.DMA((stages, PLANE)),
            pltpu.SemaphoreType.DMA((stages, PLANE)),
            pltpu.SemaphoreType.DMA((stages, ZS)),
            pltpu.SemaphoreType.DMA((stages, ZS)),
            pltpu.SemaphoreType.DMA((stages, PLANE)),
            pltpu.SemaphoreType.DMA((stages, PLANE)),
            pltpu.SemaphoreType.DMA((2, stages)),
            pltpu.SemaphoreType.DMA((steps, YS)),
            pltpu.SemaphoreType.DMA((steps, YS)),
            pltpu.SemaphoreType.DMA((steps,)),
        ],
        compiler_params=pltpu.CompilerParams(collective_id=0, has_side_effects=True, vmem_limit_bytes=48 << 20),
    )(unfolded, start_basis)
    out = pl.pallas_call(
        finish_kernel,
        out_shape=jax.ShapeDtypeStruct(y.shape, jnp.float32),
        in_specs=[pl.BlockSpec(memory_space=pltpu.VMEM)] * 2,
        out_specs=pl.BlockSpec(memory_space=pl.ANY),
        scratch_shapes=[pltpu.VMEM(y.shape, jnp.float32), pltpu.SemaphoreType.DMA((nv,))],
    )(y, factor)
    return out.reshape(nv, n2 * YS, n3 // YS, RANK)


def solution(mesh):
    in_specs = (P(None, "slab", "wide", None), P())
    out_specs = P(None, None, ("wide", "slab"), None)
    return jax.shard_map(
        per_device, mesh=mesh, in_specs=in_specs, out_specs=out_specs, check_vma=False
    )
```

time: 97 us -> 86 us (0.89)
  Pallas kernels: 93.8 us -> 82.9 us
    pallas_call x1 -> x2, Pallas kernels: 93.8 us -> 82.9 us  [the longest x1 78.4 us: per_device(): pl.pallas_call(functools.partial(tucker_kernel, nv), out_shape=[jax.Shape...]
    unnamed x1 -> x6, local copies, waits for them, and re-layouts: 3.05 us -> 2.89 us
where the time goes in v1:
time: 86 us; the launch traced here: 85.8 us
  Pallas kernels  82.9 us (96%)
  local copies, waits for them, and re-layouts  2.89 us (3%)
    pallas_call x1, Pallas kernels, per_device(): pl.pallas_call(functools.partial(tucker_kernel, nv), out_shape=[jax.Shape...  78.4 us
    pallas_call x1, Pallas kernels, per_device(): pl.pallas_call(finish_kernel, out_shape=jax.ShapeDtypeStruct(y.shape, jnp...  4.51 us
    unnamed x6, local copies, waits for them, and re-layouts  2.89 us

profile of v1, /device:TPU:1, one launch (start us, length us, event | category | flops | bytes accessed | tf_op | source)
XLA Modules:
  0.0 85.8 jit_solution(6701056757617620836)
XLA Ops:
  0.0 0.0 copy-start.1
  0.0 0.9 %copy-done.1 = f32[512,128]{1,0:T(8,128)S(1)} copy-done((f32[512,128]{1,0:T(8,128)S(1)}, f32[512,128]{1,0:T(8,128)}, u32[]{:S(2)}) %copy-start.1) | copy-done | bytes 262168
  1.0 78.4 %shard_map.28 = (f32[4,1024,128]{2,1,0:T(8,128)S(1)}, f32[128,128]{1,0:T(8,128)S(1)}) custom-call(f32[4096,512]{1,0:T(8,128)} %bitcast.2, f32[512,128]{1,0:T(8,128)S(1)} %copy-done.1), custom_call_target="tpu_custom_call" | custom-call | tf_op jit(solution)/shard_map/pallas_call | solution.py:332
  79.4 0.0 copy-start
  79.4 1.3 %copy-done = f32[4,1024,128]{2,1,0:T(8,128)} copy-done((f32[4,1024,128]{2,1,0:T(8,128)}, f32[4,1024,128]{2,1,0:T(8,128)S(1)}, u32[]{:S(2)}) %copy-start) | copy-done | bytes 2097176
  80.7 0.0 copy-start.2
  80.7 0.6 copy-done.2
  81.3 4.5 %shard_map.29 = f32[4,1024,128]{2,1,0:T(8,128)} custom-call(f32[4,1024,128]{2,1,0:T(8,128)} %copy-done, f32[128,128]{1,0:T(8,128)} %copy-done.2), custom_call_target="tpu_custom_call" | custom-call | tf_op jit(solution)/shard_map/pallas_call | solution.py:367
Async XLA Ops:
  0.0 0.9 %copy-start.1 = (f32[512,128]{1,0:T(8,128)S(1)}, f32[512,128]{1,0:T(8,128)}, u32[]{:S(2)}) copy-start(f32[512,128]{1,0:T(8,128)} %start_ref.1) | copy-start | bytes 786436
  79.4 1.3 %copy-start = (f32[4,1024,128]{2,1,0:T(8,128)}, f32[4,1024,128]{2,1,0:T(8,128)S(1)}, u32[]{:S(2)}) copy-start(f32[4,1024,128]{2,1,0:T(8,128)S(1)} %get-tuple-element.7.y_ref) | copy-start | bytes 6291460
  80.7 0.6 copy-start.2

commit v2 on v1

--- a/solution.py
+++ b/solution.py
@@ -19,6 +19,7 @@
 GROUPS = ((0, 3), (3, HALF))
 CHUNK = 512
 SUB = 8
+RAW = 2
 RANK = 128
 HIGHEST = lax.Precision.HIGHEST
 NT = (((1,), (1,)), ((), ()))
@@ -72,9 +73,9 @@
     return rows
 
 
-def tucker_kernel(nv, x_hbm, start_ref, y_ref, factor_ref, xbuf, g_ref, basis_ref, block_ref, last_ref, product_ref, outbox, s_ref, mine,
+def tucker_kernel(nv, x_hbm, start_hbm, y_ref, factor_hbm, xbuf, start_ref, factor_ref, rawbox, rawin, g_ref, basis_ref, block_ref, last_ref, product_ref, outbox, s_ref, mine,
                   theirs, inbox, total, parts, zparts, load_sem, swap_sem, rs_send, rs_recv, z_send, z_recv, ag_send, ag_recv,
-                  back_sem, out_send, out_recv, keep_sem):
+                  back_sem, out_send, out_recv, keep_sem, side_sem, raw_send, raw_recv):
     wide = lax.axis_index("wide")
     y = lax.axis_index("slab")
     core = wide % CORES
@@ -109,8 +110,9 @@
 
     for c in range(steps):
         load(c).start()
+    load_start = pltpu.make_async_copy(start_hbm, start_ref, side_sem.at[0])
+    load_start.start()
     s_ref[...] = jnp.zeros_like(s_ref)
-    basis_ref[...] = start_ref[...].T
 
     @pl.loop(0, steps)
     def _(c):
@@ -120,6 +122,28 @@
         low = (value - high.astype(jnp.float32)).astype(jnp.bfloat16)
         s_ref[...] += 0.5 * lax.dot_general(high, high, TN, preferred_element_type=jnp.float32) + lax.dot_general(
             high, low, TN, preferred_element_type=jnp.float32)
+
+    load_start.wait()
+    basis_ref[...] = start_ref[...].T
+    width = 2 * YS
+    count = CHUNK // width
+    pairs = CHUNK // YS
+    halves = steps // nv
+
+    def sort_raw(r):
+        for k in range(N1 // TILE):
+            product_ref[...] = xbuf[r * CHUNK:(r + 1) * CHUNK, k * TILE:(k + 1) * TILE]
+            for p in range(YS):
+                for i in range(2):
+                    rawbox[r, p, k, pl.ds(i, count, stride=2), :] = product_ref[pl.ds(2 * p + i, count, stride=width), :]
+
+    def raw(r, p, source):
+        return pltpu.make_async_remote_copy(
+            rawbox.at[r, p], rawin.at[r, source], raw_send.at[r, p], raw_recv.at[r, source], device_id=(wide, p), device_id_type=MESH)
+
+    def send_raw(r):
+        for d in (2, 1, 3):
+            raw(r, (y + d) % YS, y).start()
 
     scale = 1.0 / (rows * PLANE * ZS * CORES)
     pl.semaphore_wait(barrier, PLANE + ZS - 1)
@@ -158,6 +182,8 @@
         def _():
             for n in range(HALF):
                 mine[n * TILE:(n + 1) * TILE, :] = block(c * HALF + n)
+    for r in range(RAW):
+        sort_raw(r)
 
     def scatter(g, p, source):
         return pltpu.make_async_remote_copy(
@@ -200,6 +226,8 @@
         @pl.loop(1, ZS)
         def _(d):
             along_z(g, (z + d) % ZS, z).start()
+
+    send_raw(0)
 
     for g in groups:
         @pl.loop(1, ZS)
@@ -221,6 +249,9 @@
             gather(g, (me + d) % PLANE, (me + PLANE - d) % PLANE).wait_recv()
 
         back(g, core).start()
+
+    for r in range(1, RAW):
+        send_raw(r)
 
     for g in groups:
         back(g, 1 - core).wait_recv()
@@ -247,9 +278,6 @@
 
     block_ref[...] = times(basis_ref[...], g_ref[...], NN)
     last_ref[...] = times(block_ref[...], g_ref[...], NN)
-    pairs = CHUNK // YS
-    halves = steps // nv
-
     def place(c, source):
         return y_ref.at[c // halves, pl.ds((source * halves + c % halves) * pairs, pairs)]
 
@@ -258,14 +286,15 @@
             outbox.at[p, pl.ds(c * pairs, pairs)], place(c, source), out_send.at[c, p], out_recv.at[c, source],
             device_id=(wide, p), device_id_type=MESH)
 
+    def arrived(r, source):
+        return pltpu.make_async_copy(outbox.at[source, pl.ds(r * pairs, pairs)], place(r, source), out_recv.at[r, source])
+
     def keep(c):
         return pltpu.make_async_copy(outbox.at[y, pl.ds(c * pairs, pairs)], place(c, y), keep_sem.at[c])
 
-    @pl.loop(0, steps)
+    @pl.loop(RAW, steps)
     def _(c):
         product_ref[...] = times(xbuf[pl.ds(pl.multiple_of(c * CHUNK, CHUNK), CHUNK), :], last_ref[...], NT)
-        width = 2 * YS
-        count = CHUNK // width
         for p in range(YS):
             for i in range(2):
                 outbox[p, pl.ds(c * pairs + i, count, stride=2), :] = product_ref[pl.ds(2 * p + i, count, stride=width), :]
@@ -273,6 +302,15 @@
             send(c, (y + d) % YS, y).start()
         keep(c).start()
 
+    for r in range(RAW):
+        rawin[r, y] = rawbox[r, y]
+        for d in (2, 1, 3):
+            raw(r, (y + d) % YS, (y + YS - d) % YS).wait_recv()
+        for source in range(YS):
+            outbox[source, r * pairs:(r + 1) * pairs, :] = times(
+                jnp.concatenate([rawin[r, source, k] for k in range(N1 // TILE)], axis=1), last_ref[...], NT)
+            arrived(r, source).start()
+
     factor_ref[...] = jnp.zeros_like(factor_ref)
 
     @pl.loop(0, 2)
@@ -302,25 +340,62 @@
         def _(d):
             along_z(g, (z + d) % ZS, z).wait_send()
 
-    @pl.loop(0, steps)
+    store_factor = pltpu.make_async_copy(factor_ref, factor_hbm, side_sem.at[1])
+    store_factor.start()
+    for r in range(RAW):
+        for d in (2, 1, 3):
+            raw(r, (y + d) % YS, y).wait_send()
+        for source in range(YS):
+            arrived(r, source).wait()
+
+    @pl.loop(RAW, steps)
     def _(c):
         keep(c).wait()
         for d in (2, 1, 3):
             send(c, (y + d) % YS, y).wait_send()
             send(c, (y + d) % YS, (y + YS - d) % YS).wait_recv()
 
-
-def finish_kernel(y_ref, factor_ref, out_hbm, out_ref, sem):
-    nv = y_ref.shape[0]
-
-    def store(v):
-        return pltpu.make_async_copy(out_ref.at[v], out_hbm.at[v], sem.at[v])
-
-    for v in range(nv):
-        out_ref[v] = lax.dot_general(y_ref[v], factor_ref[...], NT, precision=HIGHEST, preferred_element_type=jnp.float32)
-        store(v).start()
-    for v in range(nv):
-        store(v).wait()
+    store_factor.wait()
+
+
+def three(value):
+    high = value.astype(jnp.bfloat16)
+    rest = value - high.astype(jnp.float32)
+    middle = rest.astype(jnp.bfloat16)
+    return high, middle, (rest - middle.astype(jnp.float32)).astype(jnp.bfloat16)
+
+
+def finish_kernel(y_hbm, factor_hbm, out_hbm, y_ref, factor_ref, out_ref, sem, factor_sem):
+    steps, rows = y_ref.shape[:2]
+
+    def load(c):
+        return pltpu.make_async_copy(y_hbm.at[c], y_ref.at[c], sem.at[0, c])
+
+    def store(c):
+        return pltpu.make_async_copy(out_ref.at[c], out_hbm.at[c], sem.at[1, c])
+
+    load_factor = pltpu.make_async_copy(factor_hbm, factor_ref, factor_sem)
+    load_factor.start()
+    for c in range(steps):
+        load(c).start()
+    load_factor.wait()
+    high, middle, low = three(factor_ref[...])
+    stacked = jnp.concatenate([jnp.concatenate([high, middle], axis=0)] * 2, axis=1)
+    rest = jnp.concatenate([low, high], axis=1)
+
+    @pl.loop(0, steps)
+    def _(c):
+        load(c).wait()
+        high, middle, low = three(y_ref[c])
+        first = lax.dot_general(
+            jnp.concatenate([high, middle], axis=1), stacked, NT, preferred_element_type=jnp.float32)
+        second = lax.dot_general(jnp.concatenate([high, low], axis=1), rest, NT, preferred_element_type=jnp.float32)
+        out_ref[c] = first[:, :RANK] + (first[:, RANK:] + second)
+        store(c).start()
+
+    @pl.loop(0, steps)
+    def _(c):
+        store(c).wait()
 
 
 def per_device(fields, start_basis):
@@ -332,10 +407,14 @@
     y, factor = pl.pallas_call(
         functools.partial(tucker_kernel, nv),
         out_shape=[jax.ShapeDtypeStruct((nv, rows // nv, RANK), jnp.float32), jax.ShapeDtypeStruct((RANK, RANK), jnp.float32)],
-        in_specs=[pl.BlockSpec(memory_space=pl.ANY), pl.BlockSpec(memory_space=pltpu.VMEM)],
-        out_specs=[pl.BlockSpec(memory_space=pl.ANY), pl.BlockSpec(memory_space=pltpu.VMEM)],
+        in_specs=[pl.BlockSpec(memory_space=pltpu.HBM)] * 2,
+        out_specs=[pl.BlockSpec(memory_space=pltpu.HBM)] * 2,
         scratch_shapes=[
             pltpu.VMEM((rows, n1), jnp.float32),
+            pltpu.VMEM((n1, RANK), jnp.float32),
+            pltpu.VMEM((RANK, RANK), jnp.float32),
+            pltpu.VMEM((RAW, YS, n1 // TILE, CHUNK // YS, TILE), jnp.float32),
+            pltpu.VMEM((RAW, YS, n1 // TILE, CHUNK // YS, TILE), jnp.float32),
             pltpu.VMEM((n1, n1), jnp.float32),
             pltpu.VMEM((RANK, n1), jnp.float32),
             pltpu.VMEM((RANK, n1), jnp.float32),
@@ -361,16 +440,26 @@
             pltpu.SemaphoreType.DMA((steps, YS)),
             pltpu.SemaphoreType.DMA((steps, YS)),
             pltpu.SemaphoreType.DMA((steps,)),
+            pltpu.SemaphoreType.DMA((2,)),
+            pltpu.SemaphoreType.DMA((RAW, YS)),
+            pltpu.SemaphoreType.DMA((RAW, YS)),
         ],
-        compiler_params=pltpu.CompilerParams(collective_id=0, has_side_effects=True, vmem_limit_bytes=48 << 20),
+        compiler_params=pltpu.CompilerParams(collective_id=0, has_side_effects=True, vmem_limit_bytes=67043328),
     )(unfolded, start_basis)
+    parts = (steps, CHUNK, RANK)
     out = pl.pallas_call(
         finish_kernel,
-        out_shape=jax.ShapeDtypeStruct(y.shape, jnp.float32),
-        in_specs=[pl.BlockSpec(memory_space=pltpu.VMEM)] * 2,
-        out_specs=pl.BlockSpec(memory_space=pl.ANY),
-        scratch_shapes=[pltpu.VMEM(y.shape, jnp.float32), pltpu.SemaphoreType.DMA((nv,))],
-    )(y, factor)
+        out_shape=jax.ShapeDtypeStruct(parts, jnp.float32),
+        in_specs=[pl.BlockSpec(memory_space=pltpu.HBM)] * 2,
+        out_specs=pl.BlockSpec(memory_space=pltpu.HBM),
+        scratch_shapes=[
+            pltpu.VMEM(parts, jnp.float32),
+            pltpu.VMEM((RANK, RANK), jnp.float32),
+            pltpu.VMEM(parts, jnp.float32),
+            pltpu.SemaphoreType.DMA((2, steps)),
+            pltpu.SemaphoreType.DMA,
+        ],
+    )(y.reshape(parts), factor)
     return out.reshape(nv, n2 * YS, n3 // YS, RANK)
 
 

time: 86 us -> 80.1 us (0.931)
  Pallas kernels: 82.9 us -> 79.9 us
  local copies, waits for them, and re-layouts: 2.89 us -> 0 us
    pallas_call x1, Pallas kernels: 78.4 us -> 75 us  [per_device(): pl.pallas_call(functools.partial(tucker_kernel, nv), out_shape=[jax.Shape...]
    unnamed x6 -> x0, local copies, waits for them, and re-layouts: 2.89 us -> none
where the time goes in v2:
time: 80.1 us; the launch traced here: 80 us
  Pallas kernels  79.9 us (100%)
    pallas_call x1, Pallas kernels, per_device(): pl.pallas_call(functools.partial(tucker_kernel, nv), out_shape=[jax.Shape...  75 us
    pallas_call x1, Pallas kernels, per_device(): pl.pallas_call(finish_kernel, out_shape=jax.ShapeDtypeStruct(parts, jnp.f...  4.9 us

profile of v2, /device:TPU:1, one launch (start us, length us, event | category | flops | bytes accessed | tf_op | source)
XLA Modules:
  0.0 80.0 jit_solution(5207277308433237578)
XLA Ops:
  0.0 75.0 %shard_map.28 = (f32[4,1024,128]{2,1,0:T(8,128)}, f32[128,128]{1,0:T(8,128)}) custom-call(f32[4096,512]{1,0:T(8,128)} %bitcast.3, f32[512,128]{1,0:T(8,128)} %start_hbm.1), custom_call_target="tpu_custom_call" | custom-call | tf_op jit(solution)/shard_map/pallas_call | solution.py:407
  75.0 4.9 %shard_map.29 = f32[8,512,128]{2,1,0:T(8,128)} custom-call(f32[8,512,128]{2,1,0:T(8,128)} %bitcast.4, f32[128,128]{1,0:T(8,128)} %get-tuple-element.8.factor_hbm), custom_call_target="tpu_custom_call" | custom-call | tf_op jit(solution)/shard_map/pallas_call | solution.py:450

commit v3 on v2

--- a/solution.py
+++ b/solution.py
@@ -20,6 +20,9 @@
 CHUNK = 512
 SUB = 8
 RAW = 2
+Z_STEPS = (1, -1, -3, 3)
+Z_SOURCE = (0, 0, 3, 4)
+Z_TARGET = (1, 2, 5, 6)
 RANK = 128
 HIGHEST = lax.Precision.HIGHEST
 NT = (((1,), (1,)), ((), ()))
@@ -73,9 +76,16 @@
     return rows
 
 
-def tucker_kernel(nv, x_hbm, start_hbm, y_ref, factor_hbm, xbuf, start_ref, factor_ref, rawbox, rawin, g_ref, basis_ref, block_ref, last_ref, product_ref, outbox, s_ref, mine,
+def three(value):
+    high = value.astype(jnp.bfloat16)
+    rest = value - high.astype(jnp.float32)
+    middle = rest.astype(jnp.bfloat16)
+    return high, middle, (rest - middle.astype(jnp.float32)).astype(jnp.bfloat16)
+
+
+def tucker_kernel(nv, x_hbm, start_hbm, out_hbm, xbuf, y_ref, out_ref, start_ref, factor_ref, rawbox, rawin, g_ref, basis_ref, block_ref, last_ref, product_ref, outbox, s_ref, mine,
                   theirs, inbox, total, parts, zparts, load_sem, swap_sem, rs_send, rs_recv, z_send, z_recv, ag_send, ag_recv,
-                  back_sem, out_send, out_recv, keep_sem, side_sem, raw_send, raw_recv):
+                  back_sem, out_send, out_recv, store_sem, side_sem, raw_send, raw_recv):
     wide = lax.axis_index("wide")
     y = lax.axis_index("slab")
     core = wide % CORES
@@ -98,9 +108,8 @@
     def _(d):
         pl.semaphore_signal(barrier, inc=1, device_id=plane_device((me + d) % PLANE), device_id_type=MESH)
 
-    @pl.loop(1, ZS)
-    def _(d):
-        pl.semaphore_signal(barrier, inc=1, device_id=z_device((z + d) % ZS), device_id_type=MESH)
+    for step in Z_STEPS:
+        pl.semaphore_signal(barrier, inc=1, device_id=z_device((z + ZS + step) % ZS), device_id_type=MESH)
 
     rows = x_hbm.shape[0]
     steps = rows // CHUNK
@@ -146,7 +155,7 @@
             raw(r, (y + d) % YS, y).start()
 
     scale = 1.0 / (rows * PLANE * ZS * CORES)
-    pl.semaphore_wait(barrier, PLANE + ZS - 1)
+    pl.semaphore_wait(barrier, PLANE + len(Z_STEPS))
 
     def block(n):
         i, j = PAIRS[n]
@@ -190,10 +199,10 @@
             mine.at[owned(g, p)], parts.at[source, share(g)], rs_send.at[g, p], rs_recv.at[g, source],
             device_id=plane_device(p), device_id_type=MESH)
 
-    def along_z(g, q, source):
-        return pltpu.make_async_remote_copy(
-            zparts.at[source, share(g)], zparts.at[source, share(g)], z_send.at[g, q], z_recv.at[g, source],
-            device_id=z_device(q), device_id_type=MESH)
+    def along_z(g, n):
+        return pltpu.make_async_remote_copy(
+            zparts.at[Z_SOURCE[n], share(g)], zparts.at[Z_TARGET[n], share(g)], z_send.at[g, n], z_recv.at[g, n],
+            device_id=z_device((z + ZS + Z_STEPS[n]) % ZS), device_id_type=MESH)
 
     done = total.at[core]
 
@@ -215,28 +224,32 @@
             scatter(g, (me + d) % PLANE, me).start()
 
     for g in groups:
-        zparts[z, share(g), :] = mine[owned(g, me), :]
+        zparts[0, share(g), :] = mine[owned(g, me), :]
 
         @pl.loop(1, PLANE)
         def _(d):
             source = (me + PLANE - d) % PLANE
             scatter(g, (me + d) % PLANE, source).wait_recv()
-            zparts[z, share(g), :] += parts[source, share(g), :]
-
-        @pl.loop(1, ZS)
-        def _(d):
-            along_z(g, (z + d) % ZS, z).start()
+            zparts[0, share(g), :] += parts[source, share(g), :]
+
+        for n in (0, 1):
+            along_z(g, n).start()
 
     send_raw(0)
 
     for g in groups:
-        @pl.loop(1, ZS)
-        def _(d):
-            along_z(g, (z + d) % ZS, (z + ZS - d) % ZS).wait_recv()
-
-        value = zparts[0, share(g), :]
-        for q in range(1, ZS):
-            value = value + zparts[q, share(g), :]
+        for n in (0, 1):
+            along_z(g, n).wait_recv()
+        two = zparts[0, share(g), :] + zparts[2, share(g), :]
+        zparts[4, share(g), :] = two
+        zparts[3, share(g), :] = two + zparts[1, share(g), :]
+        for n in (2, 3):
+            along_z(g, n).start()
+
+    for g in groups:
+        for n in (2, 3):
+            along_z(g, n).wait_recv()
+        value = zparts[3, share(g), :] + (zparts[5, share(g), :] + zparts[6, share(g), :])
         done[owned(g, me), :] = value
 
         @pl.loop(1, PLANE)
@@ -286,12 +299,6 @@
             outbox.at[p, pl.ds(c * pairs, pairs)], place(c, source), out_send.at[c, p], out_recv.at[c, source],
             device_id=(wide, p), device_id_type=MESH)
 
-    def arrived(r, source):
-        return pltpu.make_async_copy(outbox.at[source, pl.ds(r * pairs, pairs)], place(r, source), out_recv.at[r, source])
-
-    def keep(c):
-        return pltpu.make_async_copy(outbox.at[y, pl.ds(c * pairs, pairs)], place(c, y), keep_sem.at[c])
-
     @pl.loop(RAW, steps)
     def _(c):
         product_ref[...] = times(xbuf[pl.ds(pl.multiple_of(c * CHUNK, CHUNK), CHUNK), :], last_ref[...], NT)
@@ -300,16 +307,17 @@
                 outbox[p, pl.ds(c * pairs + i, count, stride=2), :] = product_ref[pl.ds(2 * p + i, count, stride=width), :]
         for d in (2, 1, 3):
             send(c, (y + d) % YS, y).start()
-        keep(c).start()
+        y_ref[c // halves, pl.ds(pl.multiple_of((y * halves + c % halves) * pairs, pairs), pairs), :] = outbox[
+            y, pl.ds(pl.multiple_of(c * pairs, pairs), pairs), :]
 
     for r in range(RAW):
         rawin[r, y] = rawbox[r, y]
         for d in (2, 1, 3):
             raw(r, (y + d) % YS, (y + YS - d) % YS).wait_recv()
         for source in range(YS):
-            outbox[source, r * pairs:(r + 1) * pairs, :] = times(
+            first = (source * halves + r % halves) * pairs
+            y_ref[r // halves, first:first + pairs, :] = times(
                 jnp.concatenate([rawin[r, source, k] for k in range(N1 // TILE)], axis=1), last_ref[...], NT)
-            arrived(r, source).start()
 
     factor_ref[...] = jnp.zeros_like(factor_ref)
 
@@ -336,65 +344,70 @@
             scatter(g, p, me).wait_send()
             gather(g, p, me).wait_send()
 
-        @pl.loop(1, ZS)
-        def _(d):
-            along_z(g, (z + d) % ZS, z).wait_send()
-
-    store_factor = pltpu.make_async_copy(factor_ref, factor_hbm, side_sem.at[1])
-    store_factor.start()
-    for r in range(RAW):
-        for d in (2, 1, 3):
-            raw(r, (y + d) % YS, y).wait_send()
-        for source in range(YS):
-            arrived(r, source).wait()
-
-    @pl.loop(RAW, steps)
-    def _(c):
-        keep(c).wait()
-        for d in (2, 1, 3):
-            send(c, (y + d) % YS, y).wait_send()
-            send(c, (y + d) % YS, (y + YS - d) % YS).wait_recv()
-
-    store_factor.wait()
-
-
-def three(value):
-    high = value.astype(jnp.bfloat16)
-    rest = value - high.astype(jnp.float32)
-    middle = rest.astype(jnp.bfloat16)
-    return high, middle, (rest - middle.astype(jnp.float32)).astype(jnp.bfloat16)
-
-
-def finish_kernel(y_hbm, factor_hbm, out_hbm, y_ref, factor_ref, out_ref, sem, factor_sem):
-    steps, rows = y_ref.shape[:2]
-
-    def load(c):
-        return pltpu.make_async_copy(y_hbm.at[c], y_ref.at[c], sem.at[0, c])
-
-    def store(c):
-        return pltpu.make_async_copy(out_ref.at[c], out_hbm.at[c], sem.at[1, c])
-
-    load_factor = pltpu.make_async_copy(factor_hbm, factor_ref, factor_sem)
-    load_factor.start()
-    for c in range(steps):
-        load(c).start()
-    load_factor.wait()
+        for n in range(len(Z_STEPS)):
+            along_z(g, n).wait_send()
+
     high, middle, low = three(factor_ref[...])
     stacked = jnp.concatenate([jnp.concatenate([high, middle], axis=0)] * 2, axis=1)
     rest = jnp.concatenate([low, high], axis=1)
 
+    def part(c, source):
+        return pl.ds(pl.multiple_of((source * halves + c % halves) * pairs, pairs), pairs)
+
+    def store(c, source):
+        return pltpu.make_async_copy(
+            out_ref.at[c // halves, part(c, source)], out_hbm.at[c // halves, part(c, source)], store_sem.at[c, source])
+
+    def finish(c):
+        value = jnp.concatenate([y_ref[c // halves, part(c, source), :] for source in range(YS)], axis=0)
+        high_, middle_, low_ = three(value)
+        first = lax.dot_general(jnp.concatenate([high_, middle_], axis=1), stacked, NT, preferred_element_type=jnp.float32)
+        second = lax.dot_general(jnp.concatenate([high_, low_], axis=1), rest, NT, preferred_element_type=jnp.float32)
+        value = first[:, :RANK] + (first[:, RANK:] + second)
+        for source in range(YS):
+            out_ref[c // halves, part(c, source), :] = value[source * pairs:(source + 1) * pairs, :]
+            store(c, source).start()
+
+    @pl.loop(0, RAW)
+    def _(r):
+        finish(r)
+
+    @pl.loop(RAW, steps)
+    def _(c):
+        for d in (2, 1, 3):
+            send(c, (y + d) % YS, (y + YS - d) % YS).wait_recv()
+        finish(c)
+
+    for r in range(RAW):
+        for d in (2, 1, 3):
+            raw(r, (y + d) % YS, y).wait_send()
+
+    @pl.loop(RAW, steps)
+    def _(c):
+        for d in (2, 1, 3):
+            send(c, (y + d) % YS, y).wait_send()
+
     @pl.loop(0, steps)
     def _(c):
+        for source in range(YS):
+            store(c, source).wait()
+
+
+def copy_kernel(y_hbm, out_hbm, y_ref, sem):
+    steps = y_ref.shape[0]
+
+    def load(c):
+        return pltpu.make_async_copy(y_hbm.at[c], y_ref.at[c], sem.at[0, c])
+
+    def store(c):
+        return pltpu.make_async_copy(y_ref.at[c], out_hbm.at[c], sem.at[1, c])
+
+    for c in range(steps):
+        load(c).start()
+    for c in range(steps):
         load(c).wait()
-        high, middle, low = three(y_ref[c])
-        first = lax.dot_general(
-            jnp.concatenate([high, middle], axis=1), stacked, NT, preferred_element_type=jnp.float32)
-        second = lax.dot_general(jnp.concatenate([high, low], axis=1), rest, NT, preferred_element_type=jnp.float32)
-        out_ref[c] = first[:, :RANK] + (first[:, RANK:] + second)
         store(c).start()
-
-    @pl.loop(0, steps)
-    def _(c):
+    for c in range(steps):
         store(c).wait()
 
 
@@ -404,13 +417,15 @@
     rows = unfolded.shape[0]
     steps = rows // CHUNK
     stages = len(GROUPS)
-    y, factor = pl.pallas_call(
+    y = pl.pallas_call(
         functools.partial(tucker_kernel, nv),
-        out_shape=[jax.ShapeDtypeStruct((nv, rows // nv, RANK), jnp.float32), jax.ShapeDtypeStruct((RANK, RANK), jnp.float32)],
+        out_shape=jax.ShapeDtypeStruct((nv, rows // nv, RANK), jnp.float32),
         in_specs=[pl.BlockSpec(memory_space=pltpu.HBM)] * 2,
-        out_specs=[pl.BlockSpec(memory_space=pltpu.HBM)] * 2,
+        out_specs=pl.BlockSpec(memory_space=pltpu.HBM),
         scratch_shapes=[
             pltpu.VMEM((rows, n1), jnp.float32),
+            pltpu.VMEM((nv, rows // nv, RANK), jnp.float32),
+            pltpu.VMEM((nv, rows // nv, RANK), jnp.float32),
             pltpu.VMEM((n1, RANK), jnp.float32),
             pltpu.VMEM((RANK, RANK), jnp.float32),
             pltpu.VMEM((RAW, YS, n1 // TILE, CHUNK // YS, TILE), jnp.float32),
@@ -427,39 +442,33 @@
             pltpu.VMEM((HALF * TILE, TILE), jnp.float32),
             pltpu.VMEM((CORES, HALF * TILE, TILE), jnp.float32),
             pltpu.VMEM((PLANE, HALF * OWN, TILE), jnp.float32),
-            pltpu.VMEM((ZS, HALF * OWN, TILE), jnp.float32),
+            pltpu.VMEM((7, HALF * OWN, TILE), jnp.float32),
             pltpu.SemaphoreType.DMA((steps,)),
             pltpu.SemaphoreType.DMA((2, stages)),
             pltpu.SemaphoreType.DMA((stages, PLANE)),
             pltpu.SemaphoreType.DMA((stages, PLANE)),
-            pltpu.SemaphoreType.DMA((stages, ZS)),
-            pltpu.SemaphoreType.DMA((stages, ZS)),
+            pltpu.SemaphoreType.DMA((stages, len(Z_STEPS))),
+            pltpu.SemaphoreType.DMA((stages, len(Z_STEPS))),
             pltpu.SemaphoreType.DMA((stages, PLANE)),
             pltpu.SemaphoreType.DMA((stages, PLANE)),
             pltpu.SemaphoreType.DMA((2, stages)),
             pltpu.SemaphoreType.DMA((steps, YS)),
             pltpu.SemaphoreType.DMA((steps, YS)),
-            pltpu.SemaphoreType.DMA((steps,)),
-            pltpu.SemaphoreType.DMA((2,)),
+            pltpu.SemaphoreType.DMA((steps, YS)),
+            pltpu.SemaphoreType.DMA((1,)),
             pltpu.SemaphoreType.DMA((RAW, YS)),
             pltpu.SemaphoreType.DMA((RAW, YS)),
         ],
         compiler_params=pltpu.CompilerParams(collective_id=0, has_side_effects=True, vmem_limit_bytes=67043328),
     )(unfolded, start_basis)
-    parts = (steps, CHUNK, RANK)
+    parts = (2, rows // 2, RANK)
     out = pl.pallas_call(
-        finish_kernel,
+        copy_kernel,
         out_shape=jax.ShapeDtypeStruct(parts, jnp.float32),
-        in_specs=[pl.BlockSpec(memory_space=pltpu.HBM)] * 2,
+        in_specs=[pl.BlockSpec(memory_space=pltpu.HBM)],
         out_specs=pl.BlockSpec(memory_space=pltpu.HBM),
-        scratch_shapes=[
-            pltpu.VMEM(parts, jnp.float32),
-            pltpu.VMEM((RANK, RANK), jnp.float32),
-            pltpu.VMEM(parts, jnp.float32),
-            pltpu.SemaphoreType.DMA((2, steps)),
-            pltpu.SemaphoreType.DMA,
-        ],
-    )(y.reshape(parts), factor)
+        scratch_shapes=[pltpu.VMEM(parts, jnp.float32), pltpu.SemaphoreType.DMA((2, 2))],
+    )(y.reshape(parts))
     return out.reshape(nv, n2 * YS, n3 // YS, RANK)
 
 

time: 80.1 us -> 80 us (level)
  no operation moved by 1% of the time
where the time goes in v3:
time: 80 us; the launch traced here: 79.9 us
  Pallas kernels  79.7 us (100%)
    pallas_call x1, Pallas kernels, per_device(): pl.pallas_call(functools.partial(tucker_kernel, nv), out_shape=jax.ShapeD...  77.1 us
    pallas_call x1, Pallas kernels, per_device(): pl.pallas_call(copy_kernel, out_shape=jax.ShapeDtypeStruct(parts, jnp.flo...  2.57 us

profile of v3, /device:TPU:1, one launch (start us, length us, event | category | flops | bytes accessed | tf_op | source)
XLA Modules:
  0.0 79.9 jit_solution(16005295298740301022)
XLA Ops:
  0.0 77.1 %shard_map.28 = f32[4,1024,128]{2,1,0:T(8,128)} custom-call(f32[4096,512]{1,0:T(8,128)} %bitcast.3, f32[512,128]{1,0:T(8,128)} %start_hbm.1), custom_call_target="tpu_custom_call" | custom-call | tf_op jit(solution)/shard_map/pallas_call | solution.py:420
  77.1 2.6 %shard_map.29 = f32[2,2048,128]{2,1,0:T(8,128)} custom-call(f32[2,2048,128]{2,1,0:T(8,128)} %bitcast.4), custom_call_target="tpu_custom_call" | custom-call | tf_op jit(solution)/shard_map/pallas_call | solution.py:465

commit v4 on v3

--- a/solution.py
+++ b/solution.py
@@ -83,7 +83,7 @@
     return high, middle, (rest - middle.astype(jnp.float32)).astype(jnp.bfloat16)
 
 
-def tucker_kernel(nv, x_hbm, start_hbm, out_hbm, xbuf, y_ref, out_ref, start_ref, factor_ref, rawbox, rawin, g_ref, basis_ref, block_ref, last_ref, product_ref, outbox, s_ref, mine,
+def tucker_kernel(nv, x_hbm, start_hbm, out_hbm, xbuf, y_ref, out_ref, start_ref, factor_ref, rawbox, rawin, g_ref, basis_ref, block_ref, last_ref, wide_ref, deep_ref, product_ref, outbox, s_ref, mine,
                   theirs, inbox, total, parts, zparts, load_sem, swap_sem, rs_send, rs_recv, z_send, z_recv, ag_send, ag_recv,
                   back_sem, out_send, out_recv, store_sem, side_sem, raw_send, raw_recv):
     wide = lax.axis_index("wide")
@@ -291,6 +291,17 @@
 
     block_ref[...] = times(basis_ref[...], g_ref[...], NN)
     last_ref[...] = times(block_ref[...], g_ref[...], NN)
+    high, middle, low = three(last_ref[...].T)
+    wide_ref[...] = jnp.concatenate([high, middle], axis=1)
+    deep_ref[...] = jnp.concatenate([low, high], axis=0)
+
+    def by_last(value):
+        high, middle, low = three(value)
+        both = lax.dot_general(high, wide_ref[...], NN, preferred_element_type=jnp.float32) + lax.dot_general(
+            middle, wide_ref[...], NN, preferred_element_type=jnp.float32)
+        return both[:, :RANK] + (both[:, RANK:] + lax.dot_general(
+            jnp.concatenate([high, low], axis=1), deep_ref[...], NN, preferred_element_type=jnp.float32))
+
     def place(c, source):
         return y_ref.at[c // halves, pl.ds((source * halves + c % halves) * pairs, pairs)]
 
@@ -301,7 +312,7 @@
 
     @pl.loop(RAW, steps)
     def _(c):
-        product_ref[...] = times(xbuf[pl.ds(pl.multiple_of(c * CHUNK, CHUNK), CHUNK), :], last_ref[...], NT)
+        product_ref[...] = by_last(xbuf[pl.ds(pl.multiple_of(c * CHUNK, CHUNK), CHUNK), :])
         for p in range(YS):
             for i in range(2):
                 outbox[p, pl.ds(c * pairs + i, count, stride=2), :] = product_ref[pl.ds(2 * p + i, count, stride=width), :]
@@ -314,10 +325,11 @@
         rawin[r, y] = rawbox[r, y]
         for d in (2, 1, 3):
             raw(r, (y + d) % YS, (y + YS - d) % YS).wait_recv()
+        value = by_last(jnp.concatenate(
+            [jnp.concatenate([rawin[r, source, k] for k in range(N1 // TILE)], axis=1) for source in range(YS)], axis=0))
         for source in range(YS):
             first = (source * halves + r % halves) * pairs
-            y_ref[r // halves, first:first + pairs, :] = times(
-                jnp.concatenate([rawin[r, source, k] for k in range(N1 // TILE)], axis=1), last_ref[...], NT)
+            y_ref[r // halves, first:first + pairs, :] = value[source * pairs:(source + 1) * pairs, :]
 
     factor_ref[...] = jnp.zeros_like(factor_ref)
 
@@ -434,6 +446,8 @@
             pltpu.VMEM((RANK, n1), jnp.float32),
             pltpu.VMEM((RANK, n1), jnp.float32),
             pltpu.VMEM((RANK, n1), jnp.float32),
+            pltpu.VMEM((n1, 2 * RANK), jnp.bfloat16),
+            pltpu.VMEM((2 * n1, RANK), jnp.bfloat16),
             pltpu.VMEM((CHUNK, RANK), jnp.float32),
             pltpu.VMEM((YS, rows // YS, RANK), jnp.float32),
             pltpu.VMEM((n1, n1), jnp.float32),

time: 80 us -> 78.3 us (0.979)
  Pallas kernels: 79.7 us -> 78 us
    pallas_call x1, Pallas kernels: 77.1 us -> 75.5 us  [per_device(): pl.pallas_call(functools.partial(tucker_kernel, nv), out_shape=jax.ShapeD...]
where the time goes in v4:
time: 78.3 us; the launch traced here: 78.2 us
  Pallas kernels  78 us (100%)
    pallas_call x1, Pallas kernels, per_device(): pl.pallas_call(functools.partial(tucker_kernel, nv), out_shape=jax.ShapeD...  75.5 us
    pallas_call x1, Pallas kernels, per_device(): pl.pallas_call(copy_kernel, out_shape=jax.ShapeDtypeStruct(parts, jnp.flo...  2.57 us

profile of v4, /device:TPU:1, one launch (start us, length us, event | category | flops | bytes accessed | tf_op | source)
XLA Modules:
  0.0 78.2 jit_solution(16530908157294056715)
XLA Ops:
  0.0 75.5 %shard_map.28 = f32[4,1024,128]{2,1,0:T(8,128)} custom-call(f32[4096,512]{1,0:T(8,128)} %bitcast.3, f32[512,128]{1,0:T(8,128)} %start_hbm.1), custom_call_target="tpu_custom_call" | custom-call | tf_op jit(solution)/shard_map/pallas_call | solution.py:432
  75.5 2.6 %shard_map.29 = f32[2,2048,128]{2,1,0:T(8,128)} custom-call(f32[2,2048,128]{2,1,0:T(8,128)} %bitcast.4), custom_call_target="tpu_custom_call" | custom-call | tf_op jit(solution)/shard_map/pallas_call | solution.py:479

commit v5 on v4

--- a/solution.py
+++ b/solution.py
@@ -20,6 +20,9 @@
 CHUNK = 512
 SUB = 8
 RAW = 2
+PIECES = RAW * (N1 // TILE)
+EARLY = 2
+MIDDLE = 5
 Z_STEPS = (1, -1, -3, 3)
 Z_SOURCE = (0, 0, 3, 4)
 Z_TARGET = (1, 2, 5, 6)
@@ -123,9 +126,7 @@
     load_start.start()
     s_ref[...] = jnp.zeros_like(s_ref)
 
-    @pl.loop(0, steps)
-    def _(c):
-        load(c).wait()
+    def add_slice(c):
         value = xbuf[pl.ds(pl.multiple_of(c * CHUNK, CHUNK), CHUNK), :]
         high = value.astype(jnp.bfloat16)
         low = (value - high.astype(jnp.float32)).astype(jnp.bfloat16)
@@ -139,23 +140,38 @@
     pairs = CHUNK // YS
     halves = steps // nv
 
-    def sort_raw(r):
-        for k in range(N1 // TILE):
-            product_ref[...] = xbuf[r * CHUNK:(r + 1) * CHUNK, k * TILE:(k + 1) * TILE]
-            for p in range(YS):
-                for i in range(2):
-                    rawbox[r, p, k, pl.ds(i, count, stride=2), :] = product_ref[pl.ds(2 * p + i, count, stride=width), :]
-
-    def raw(r, p, source):
-        return pltpu.make_async_remote_copy(
-            rawbox.at[r, p], rawin.at[r, source], raw_send.at[r, p], raw_recv.at[r, source], device_id=(wide, p), device_id_type=MESH)
-
-    def send_raw(r):
-        for d in (2, 1, 3):
-            raw(r, (y + d) % YS, y).start()
+    columns = N1 // TILE
+
+    def sort_raw(n):
+        r, k = n // columns, n % columns
+        product_ref[...] = xbuf[r * CHUNK:(r + 1) * CHUNK, k * TILE:(k + 1) * TILE]
+        for p in range(YS):
+            for i in range(2):
+                rawbox[n, p, pl.ds(i, count, stride=2), :] = product_ref[pl.ds(2 * p + i, count, stride=width), :]
+
+    def raw(n, p, source):
+        return pltpu.make_async_remote_copy(
+            rawbox.at[n, p], rawin.at[n, source], raw_send.at[n, p], raw_recv.at[n, source], device_id=(wide, p), device_id_type=MESH)
+
+    def send_raw(first, last):
+        @pl.loop(first, last)
+        def _(n):
+            for d in (2, 1, 3):
+                raw(n, (y + d) % YS, y).start()
+
+    load(0).wait()
+    for n in range(EARLY):
+        sort_raw(n)
+    pl.semaphore_wait(barrier, PLANE + len(Z_STEPS))
+    send_raw(0, EARLY)
+    add_slice(0)
+
+    @pl.loop(1, steps)
+    def _(c):
+        load(c).wait()
+        add_slice(c)
 
     scale = 1.0 / (rows * PLANE * ZS * CORES)
-    pl.semaphore_wait(barrier, PLANE + len(Z_STEPS))
 
     def block(n):
         i, j = PAIRS[n]
@@ -191,8 +207,8 @@
         def _():
             for n in range(HALF):
                 mine[n * TILE:(n + 1) * TILE, :] = block(c * HALF + n)
-    for r in range(RAW):
-        sort_raw(r)
+    for n in range(EARLY, PIECES):
+        sort_raw(n)
 
     def scatter(g, p, source):
         return pltpu.make_async_remote_copy(
@@ -235,7 +251,7 @@
         for n in (0, 1):
             along_z(g, n).start()
 
-    send_raw(0)
+    send_raw(EARLY, MIDDLE)
 
     for g in groups:
         for n in (0, 1):
@@ -263,8 +279,7 @@
 
         back(g, core).start()
 
-    for r in range(1, RAW):
-        send_raw(r)
+    send_raw(MIDDLE, PIECES)
 
     for g in groups:
         back(g, 1 - core).wait_recv()
@@ -321,12 +336,15 @@
         y_ref[c // halves, pl.ds(pl.multiple_of((y * halves + c % halves) * pairs, pairs), pairs), :] = outbox[
             y, pl.ds(pl.multiple_of(c * pairs, pairs), pairs), :]
 
+    @pl.loop(0, PIECES)
+    def _(n):
+        rawin[n, y] = rawbox[n, y]
+        for d in (2, 1, 3):
+            raw(n, (y + d) % YS, (y + YS - d) % YS).wait_recv()
+
     for r in range(RAW):
-        rawin[r, y] = rawbox[r, y]
-        for d in (2, 1, 3):
-            raw(r, (y + d) % YS, (y + YS - d) % YS).wait_recv()
         value = by_last(jnp.concatenate(
-            [jnp.concatenate([rawin[r, source, k] for k in range(N1 // TILE)], axis=1) for source in range(YS)], axis=0))
+            [jnp.concatenate([rawin[r * columns + k, source] for k in range(columns)], axis=1) for source in range(YS)], axis=0))
         for source in range(YS):
             first = (source * halves + r % halves) * pairs
             y_ref[r // halves, first:first + pairs, :] = value[source * pairs:(source + 1) * pairs, :]
@@ -390,9 +408,10 @@
             send(c, (y + d) % YS, (y + YS - d) % YS).wait_recv()
         finish(c)
 
-    for r in range(RAW):
+    @pl.loop(0, PIECES)
+    def _(n):
         for d in (2, 1, 3):
-            raw(r, (y + d) % YS, y).wait_send()
+            raw(n, (y + d) % YS, y).wait_send()
 
     @pl.loop(RAW, steps)
     def _(c):
@@ -440,8 +459,8 @@
             pltpu.VMEM((nv, rows // nv, RANK), jnp.float32),
             pltpu.VMEM((n1, RANK), jnp.float32),
             pltpu.VMEM((RANK, RANK), jnp.float32),
-            pltpu.VMEM((RAW, YS, n1 // TILE, CHUNK // YS, TILE), jnp.float32),
-            pltpu.VMEM((RAW, YS, n1 // TILE, CHUNK // YS, TILE), jnp.float32),
+            pltpu.VMEM((PIECES, YS, CHUNK // YS, TILE), jnp.float32),
+            pltpu.VMEM((PIECES, YS, CHUNK // YS, TILE), jnp.float32),
             pltpu.VMEM((n1, n1), jnp.float32),
             pltpu.VMEM((RANK, n1), jnp.float32),
             pltpu.VMEM((RANK, n1), jnp.float32),
@@ -470,8 +489,8 @@
             pltpu.SemaphoreType.DMA((steps, YS)),
             pltpu.SemaphoreType.DMA((steps, YS)),
             pltpu.SemaphoreType.DMA((1,)),
-            pltpu.SemaphoreType.DMA((RAW, YS)),
-            pltpu.SemaphoreType.DMA((RAW, YS)),
+            pltpu.SemaphoreType.DMA((PIECES, YS)),
+            pltpu.SemaphoreType.DMA((PIECES, YS)),
         ],
         compiler_params=pltpu.CompilerParams(collective_id=0, has_side_effects=True, vmem_limit_bytes=67043328),
     )(unfolded, start_basis)

time: 78.3 us -> 81.8 us (1.045)
  Pallas kernels: 78 us -> 81.5 us
    pallas_call x1, Pallas kernels: 75.5 us -> 78.9 us  [per_device(): pl.pallas_call(functools.partial(tucker_kernel, nv), out_shape=jax.ShapeD...]
where the time goes in v5:
time: 81.8 us; the launch traced here: 81.7 us
  Pallas kernels  81.5 us (100%)
    pallas_call x1, Pallas kernels, per_device(): pl.pallas_call(functools.partial(tucker_kernel, nv), out_shape=jax.ShapeD...  78.9 us
    pallas_call x1, Pallas kernels, per_device(): pl.pallas_call(copy_kernel, out_shape=jax.ShapeDtypeStruct(parts, jnp.flo...  2.57 us

profile of v5, /device:TPU:1, one launch (start us, length us, event | category | flops | bytes accessed | tf_op | source)
XLA Modules:
  0.0 81.7 jit_solution(9968592443573005543)
XLA Ops:
  0.0 78.9 %shard_map.28 = f32[4,1024,128]{2,1,0:T(8,128)} custom-call(f32[4096,512]{1,0:T(8,128)} %bitcast.3, f32[512,128]{1,0:T(8,128)} %start_hbm.1), custom_call_target="tpu_custom_call" | custom-call | tf_op jit(solution)/shard_map/pallas_call | solution.py:451
  78.9 2.6 %shard_map.29 = f32[2,2048,128]{2,1,0:T(8,128)} custom-call(f32[2,2048,128]{2,1,0:T(8,128)} %bitcast.4), custom_call_target="tpu_custom_call" | custom-call | tf_op jit(solution)/shard_map/pallas_call | solution.py:498
